TPU v7x, 32 devices: a whole 2x2x4 slice. The times are simulated.
32 devices in a mesh: group: 2 (over y), tile: 16 (over z, x, core).
Axes of the slice: x: 2, y: 2, z: 4, core: 2. Of those that a mesh axis runs over, the one named last changes fastest.
Arguments:
- site_tensors: bfloat16 [16, 6, 2, 65536], P('tile', 'group'), may hold values from -6 to 6
- msg_in: float32 [16, 6, 4, 256], P('tile', 'group'), may hold values from -6 to 6
Outputs:
- new_tensors: bfloat16 [16, 6, 2, 65536], P('tile', 'group')
- messages: float32 [16, 6, 4, 256], P('tile', 'group')
All inputs are finite; a program needn't handle non-finite values.
Results may differ from a plain program's by a relative error of at most 0.029.
The roundings to bfloat16 on the way count: a program that leaves them out, or rounds other values in their place, can miss the bound.
Values may be sent and summed in bfloat16 or wider, within the bound.
A program may use at most 256 MiB of HBM per device.

v0:
```python
import functools
import math

import jax
import jax.numpy as jnp
from jax import lax
from jax.experimental import pallas as pl
from jax.experimental.pallas import tpu as pltpu
from jax.sharding import PartitionSpec as P

ITERS = 2
NS_STEPS = 6
LANES = 128
EPSILON = 1e-06
COUPLING = 0.5
FIELD = 0.3
F32 = jnp.float32
BF16 = jnp.bfloat16
MESH = pl.DeviceIdType.MESH


def iota(shape, axis):
    return lax.broadcasted_iota(jnp.int32, shape, axis)


def dot(a, b):
    return jnp.dot(a, b, preferred_element_type=F32)


def dot_nt(a, b):
    return lax.dot_general(a, b, (((1,), (1,)), ((), ())), preferred_element_type=F32)


def dot_tn(a, b):
    return lax.dot_general(a, b, (((0,), (0,)), ((), ())), preferred_element_type=F32)


def parts(value, count):
    out = []
    for _ in range(count):
        piece = value.astype(BF16)
        out.append(piece)
        value = value - piece.astype(F32)
    return out


def select_dot(value, selector, count):
    total = None
    for piece in parts(value, count):
        term = dot(piece, selector)
        total = term if total is None else total + term
    return total


def dot3(a, b):
    (a_hi, a_lo), (b_hi, b_lo) = parts(a, 2), parts(b, 2)
    return dot(a_hi, b_hi) + (dot(a_hi, b_lo) + dot(a_lo, b_hi))


def one_hot(mask):
    return jnp.where(mask, 1.0, 0.0).astype(BF16)


def kernel(tiles, groups, cols, D, a_ref, msg_ref, out_ref, mout_ref,
           x_ref, xt_ref, ax_ref, kron_ref,
           send_up, send_down, send_side, recv_up, recv_down, recv_side,
           send_sem, recv_sem):
    tile = lax.axis_index("tile")
    group = lax.axis_index("group")
    DD = D * D
    shift = D.bit_length() - 1
    halves = DD // LANES
    mixed = 2 * halves
    rows = DD // mixed
    legs = 4 * cols
    wide = legs * D
    has_up = tile > 0
    has_down = tile < tiles - 1

    barrier = pltpu.get_barrier_semaphore()

    @pl.when(has_up)
    def _():
        pl.semaphore_signal(barrier, inc=1, device_id={"tile": tile - 1}, device_id_type=MESH)

    @pl.when(has_down)
    def _():
        pl.semaphore_signal(barrier, inc=1, device_id={"tile": tile + 1}, device_id_type=MESH)

    pl.semaphore_signal(barrier, inc=1, device_id={"group": 1 - group}, device_id_type=MESH)

    lane = iota((D, DD), 1)
    row = iota((D, DD), 0)
    major = one_hot((lane >> shift) == row)
    minor = one_hot((lane & (D - 1)) == row)
    both = jnp.concatenate([major, minor], axis=1)
    major_t = one_hot((iota((DD, D), 0) >> shift) == iota((DD, D), 1))
    minor_t = one_hot((iota((DD, D), 0) & (D - 1)) == iota((DD, D), 1))

    def permutation(out_axis):
        p, k = iota((DD, DD), out_axis), iota((DD, DD), 1 - out_axis)
        row_bits = rows.bit_length() - 1
        return one_hot(k == (p & (rows - 1)) * mixed + (p >> row_bits))

    unfold_mask = (lane >> shift) == row
    flat = msg_ref[...].reshape(legs, DD)
    spread = jnp.concatenate(
        [jnp.where(unfold_mask, flat[m : m + 1, :], 0.0) for m in range(legs)], axis=0
    )
    edge_all = select_dot(spread, minor_t, 3)
    edge = [edge_all[m * D : (m + 1) * D] for m in range(legs)]

    gather = permutation(0)
    for i in range(cols):
        for b in range(DD // rows):
            block = dot(gather, a_ref[i, b * DD : (b + 1) * DD, :]).astype(BF16)
            for g in range(mixed):
                x_ref[
                    i, g % 2, b * rows : (b + 1) * rows, (g // 2) * LANES : (g // 2 + 1) * LANES
                ] = block[g * rows : (g + 1) * rows]
        for s in range(2):
            xt_ref[i, s] = x_ref[i, s].T

    def build_kron(slot, first, second):
        for d in range(D):
            kron_ref[slot, d * D : (d + 1) * D, :] = (first[d : d + 1, :] * second).astype(BF16)

    def outgoing(incoming, last):
        stacked = jnp.concatenate([v.astype(BF16) for v in incoming], axis=0)
        spread = dot(stacked, both)

        def by_major(m):
            return spread[m * D : (m + 1) * D, :DD]

        def by_minor(m):
            return spread[m * D : (m + 1) * D, DD:]

        firsts, seconds = [], []
        for i in range(cols):
            for path in range(2):
                left, right = (x_ref, xt_ref) if path == 0 else (xt_ref, x_ref)
                far = i * 4 + 2 * (1 - path)
                near = i * 4 + 2 * path
                slot = i * 2 + path
                build_kron(slot, by_major(far), by_minor(far + 1))
                near_major, near_minor = by_major(near), by_minor(near + 1)
                pair = []
                for s in range(2):
                    y = dot(left[i, s], kron_ref[slot]).astype(BF16)
                    gram = dot(y, right[i, s])
                    first = jnp.concatenate(
                        [
                            jnp.sum(
                                gram[d * D : (d + 1) * D] * near_minor, axis=0, keepdims=True
                            )
                            for d in range(D)
                        ],
                        axis=0,
                    )
                    second = gram[:D] * near_major[0:1, :]
                    for d in range(1, D):
                        second = second + gram[d * D : (d + 1) * D] * near_major[d : d + 1, :]
                    pair.append((first, second))
                firsts.append((pair[0][0] + pair[1][0], pair[0][0] - pair[1][0]))
                seconds.append((pair[0][1] + pair[1][1], pair[0][1] - pair[1][1]))
        kinds = 2 if last else 1
        reduced = []
        for kind in range(kinds):
            by_first = select_dot(jnp.concatenate([f[kind] for f in firsts], axis=0), major_t, 2)
            by_second = select_dot(jnp.concatenate([f[kind] for f in seconds], axis=0), minor_t, 2)
            blocks = []
            for slot in range(2 * cols):
                blocks.append(by_first[slot * D : (slot + 1) * D])
                blocks.append(by_second[slot * D : (slot + 1) * D])
            reduced.append(blocks)
        scales = [
            jnp.sqrt(jnp.sum(v * v, axis=(0, 1), keepdims=True) / DD + EPSILON) for v in reduced[0]
        ]
        return [[v / r for v, r in zip(blocks, scales)] for blocks in reduced]

    def exchange(turn, values):
        kinds = len(values)
        width = kinds * cols * D

        def packed(leg):
            return jnp.concatenate([b[i * 4 + leg] for b in values for i in range(cols)], axis=1)

        up_src = send_up.at[turn]
        down_src = send_down.at[turn]
        side_src = send_side.at[turn]
        send_up[turn, :, :width] = packed(0)
        send_down[turn, :, :width] = packed(2)
        side_right = jnp.concatenate([b[(cols - 1) * 4 + 3] for b in values], axis=1)
        side_left = jnp.concatenate([b[1] for b in values], axis=1)
        send_side[turn, :, : kinds * D] = jnp.where(group == 0, side_right, side_left)

        def copy(src, dst, k, device):
            return pltpu.make_async_remote_copy(
                src_ref=src, dst_ref=dst.at[turn], send_sem=send_sem.at[turn, k],
                recv_sem=recv_sem.at[turn, k], device_id=device, device_id_type=MESH,
            )

        to_up = copy(up_src, recv_down, 0, {"tile": tile - 1})
        to_down = copy(down_src, recv_up, 1, {"tile": tile + 1})
        to_side = copy(side_src, recv_side, 2, {"group": 1 - group})

        @pl.when(has_up)
        def _():
            to_up.start()

        @pl.when(has_down)
        def _():
            to_down.start()

        to_side.start()
        return to_up, to_down, to_side

    def finish(turn, copies, values):
        to_up, to_down, to_side = copies
        kinds = len(values)
        width = kinds * cols * D

        def border(leg):
            blocks = [edge[i * 4 + leg] for i in range(cols)]
            if kinds == 2:
                blocks += [jnp.zeros((D, D), F32)] * cols
            return jnp.concatenate(blocks, axis=1)

        @pl.when(has_up)
        def _():
            to_up.wait_send()
            to_down.wait_recv()

        @pl.when(jnp.logical_not(has_up))
        def _():
            recv_up[turn, :, :width] = border(0)

        @pl.when(has_down)
        def _():
            to_down.wait_send()
            to_up.wait_recv()

        @pl.when(jnp.logical_not(has_down))
        def _():
            recv_down[turn, :, :width] = border(2)

        to_side.wait()
        from_up, from_down, from_side = recv_up[turn], recv_down[turn], recv_side[turn]
        routed = []
        for kind in range(kinds):
            blocks = []
            for i in range(cols):
                at = (kind * cols + i) * D
                side = from_side[:, kind * D : (kind + 1) * D]
                zero = jnp.zeros((D, D), F32)
                out_left = edge[i * 4 + 1] if kind == 0 else zero
                out_right = edge[i * 4 + 3] if kind == 0 else zero
                blocks.append(from_up[:, at : at + D])
                if i > 0:
                    blocks.append(values[kind][(i - 1) * 4 + 3])
                else:
                    blocks.append(jnp.where(group == 0, out_left, side))
                blocks.append(from_down[:, at : at + D])
                if i < cols - 1:
                    blocks.append(values[kind][(i + 1) * 4 + 1])
                else:
                    blocks.append(jnp.where(group == groups - 1, out_right, side))
            routed.append(blocks)
        return routed

    incoming = edge
    for turn in range(ITERS):
        last = turn == ITERS - 1
        values = outgoing(incoming, last)
        if turn == 0:
            inside = jnp.logical_and(has_up, has_down)

            @pl.when(inside)
            def _():
                pl.semaphore_wait(barrier, 3)

            @pl.when(jnp.logical_not(inside))
            def _():
                pl.semaphore_wait(barrier, 2)

        copies = exchange(turn, values)
        if last:
            for i in range(cols):
                a0, a1 = x_ref[i, 0].astype(F32), x_ref[i, 1].astype(F32)
                ch, sh = math.cosh(FIELD), math.sinh(FIELD)
                ax_ref[i, 0] = (ch * a0 + sh * a1).astype(BF16)
                ax_ref[i, 1] = (ch * a1 + sh * a0).astype(BF16)
        routed = finish(turn, copies, values)
        incoming = routed[0]

    stacked = jnp.concatenate(incoming, axis=0)
    spread = select_dot(stacked, minor, 3)
    flat_rows = [
        jnp.sum(
            jnp.where(unfold_mask, spread[m * D : (m + 1) * D], 0.0), axis=0, keepdims=True
        )
        for m in range(legs)
    ]
    mout_ref[...] = jnp.concatenate(flat_rows, axis=0).reshape(cols, 4, DD)

    g0, g1 = math.cosh(COUPLING), math.sinh(COUPLING)
    cross = math.sqrt(g0 * g1)
    root2 = math.sqrt(2.0)
    msg_sum = jnp.concatenate([o + n for o, n in zip(values[0], routed[0])], axis=1)
    twist_sum = jnp.concatenate([o + n for o, n in zip(values[1], routed[1])], axis=1)
    y_top = ((g0 * msg_sum + cross * twist_sum) / root2).astype(BF16)
    y_bot = ((cross * twist_sum + g1 * msg_sum) / root2).astype(BF16)
    y_both = jnp.concatenate([y_top, y_bot], axis=0)
    r_id, c_id = iota((wide, wide), 0), iota((wide, wide), 1)
    same = (r_id >> shift) == (c_id >> shift)
    eye = jnp.where(r_id == c_id, 1.0, 0.0).astype(F32)
    gram = jnp.where(same, dot_tn(y_both, y_both), 0.0)
    diag = jnp.sum(gram * eye, axis=0, keepdims=True)
    diag8 = jnp.broadcast_to(diag, (8, wide))
    trace = select_dot(diag8, one_hot(same), 3)[0:1] + EPSILON
    current = gram / trace
    inverse = eye
    for step in range(NS_STEPS):
        if step == 0:
            factor = 1.5 * eye - 0.5 * current
            inverse_next = factor
        else:
            factor = 1.5 * eye - 0.5 * dot3(inverse, current)
            inverse_next = dot3(factor, inverse)
        if step < NS_STEPS - 1:
            current = dot3(current, factor)
        inverse = inverse_next
    q_both = dot(y_both, inverse.astype(BF16)) / jnp.sqrt(trace)
    first = math.sqrt(g0) * q_both[:D]
    second = math.sqrt(g1) * q_both[D:]
    lane_w = iota((D, wide), 1)
    leg_of = (lane_w >> shift) & 3
    col_of = (lane_w >> (shift + 2)) + group * cols
    at_edge = (
        ((leg_of == 0) & (tile == 0))
        | ((leg_of == 2) & (tile == tiles - 1))
        | ((leg_of == 1) & (col_of == 0))
        | ((leg_of == 3) & (col_of == groups * cols - 1))
    )
    unit = jnp.where((lane_w & (D - 1)) == iota((D, wide), 0), 1.0, 0.0).astype(F32)
    scatter = permutation(1)
    spreads = []
    for weight in (first + second, first - second):
        weight = jnp.where(at_edge, unit, weight)
        spreads.append(dot(weight.T.astype(BF16), both))
    for i in range(cols):
        gated = []
        for s in range(2):
            w = spreads[s]
            m = i * 4
            build_kron(0 + 2 * s, w[(m + 2) * D : (m + 3) * D, :DD], w[(m + 3) * D : (m + 4) * D, DD:])
            build_kron(1 + 2 * s, w[m * D : (m + 1) * D, :DD], w[(m + 1) * D : (m + 2) * D, DD:])
            half = dot_nt(ax_ref[i, s], kron_ref[0 + 2 * s]).astype(BF16)
            gated.append(dot(kron_ref[1 + 2 * s], half).astype(BF16))
        for b in range(DD // rows):
            block = jnp.concatenate(
                [
                    gated[g % 2][
                        b * rows : (b + 1) * rows, (g // 2) * LANES : (g // 2 + 1) * LANES
                    ]
                    for g in range(mixed)
                ],
                axis=0,
            )
            out_ref[i, b * DD : (b + 1) * DD, :] = dot(scatter, block).astype(BF16)


def per_device(tiles, groups, site_tensors, msg_in):
    _, cols, _, size = site_tensors.shape
    DD = msg_in.shape[-1]
    D = math.isqrt(DD)
    chunks = size // LANES
    a = site_tensors.reshape(cols, 2, chunks, LANES).transpose(0, 2, 1, 3)
    a = a.reshape(cols, 2 * chunks, LANES)
    wide = 2 * cols * D
    vmem = pl.BlockSpec(memory_space=pltpu.VMEM)
    out, messages = pl.pallas_call(
        functools.partial(kernel, tiles, groups, cols, D),
        out_shape=(
            jax.ShapeDtypeStruct(a.shape, BF16),
            jax.ShapeDtypeStruct((cols, 4, DD), F32),
        ),
        in_specs=[vmem, vmem],
        out_specs=(vmem, vmem),
        scratch_shapes=[
            pltpu.VMEM((cols, 2, DD, DD), BF16),
            pltpu.VMEM((cols, 2, DD, DD), BF16),
            pltpu.VMEM((cols, 2, DD, DD), BF16),
            pltpu.VMEM((max(4, 2 * cols), DD, DD), BF16),
            pltpu.VMEM((ITERS, D, wide), F32),
            pltpu.VMEM((ITERS, D, wide), F32),
            pltpu.VMEM((ITERS, D, 2 * D), F32),
            pltpu.VMEM((ITERS, D, wide), F32),
            pltpu.VMEM((ITERS, D, wide), F32),
            pltpu.VMEM((ITERS, D, 2 * D), F32),
            pltpu.SemaphoreType.DMA((ITERS, 3)),
            pltpu.SemaphoreType.DMA((ITERS, 3)),
        ],
        compiler_params=pltpu.CompilerParams(collective_id=0, has_side_effects=True),
    )(a, msg_in[0])
    out = out.reshape(cols, chunks, 2, LANES).transpose(0, 2, 1, 3)
    return out.reshape(1, cols, 2, size), messages[None]


def solution(mesh):
    spec = P("tile", "group", None, None)
    return jax.shard_map(
        functools.partial(per_device, mesh.shape["tile"], mesh.shape["group"]),
        mesh=mesh, in_specs=(spec, spec), out_specs=(spec, spec), check_vma=False,
    )
```

profile of v0, /device:TPU:1, one launch (start us, length us, event | category | flops | bytes accessed | tf_op | source)
XLA Modules:
  0.0 22.7 jit_solution(5265527120226301528)
XLA Ops:
  0.6 18.9 %shard_map.41 = (bf16[3,1024,128]{2,1,0:T(8,128)(2,1)}, f32[3,4,256]{2,1,0:T(4,128)}) custom-call(bf16[3,1024,128]{2,1,0:T(8,128)(2,1)} %bitcast.12, f32[3,4,256]{2,1,0:T(4,128)} %bitcast.15), custom_call_target="tpu_custom_call" | custom-call | tf_op jit(solution)/shard_map/pallas_call | solution.py:382
  19.5 0.0 copy-start
  19.5 2.6 %copy.8 = bf16[1,3,2,65536]{3,2,1,0:T(2,128)(2,1)} copy(bf16[1,3,2,65536]{3,2,1,0:T(2,128)(2,1)} %bitcast.13) | data formatting | bytes 1572864
  22.1 0.0 copy-done
  22.1 0.6 %copy.9 = f32[1,3,4,256]{3,2,1,0:T(4,128)} copy(f32[1,3,4,256]{3,2,1,0:T(4,128)S(1)} %bitcast.14) | data formatting | bytes 24576
Async XLA Ops:
  19.5 2.6 %copy-start = (f32[3,4,256]{2,1,0:T(4,128)S(1)}, f32[3,4,256]{2,1,0:T(4,128)}, u32[]{:S(2)}) copy-start(f32[3,4,256]{2,1,0:T(4,128)} %get-tuple-element.5) | copy-start | bytes 36868
where the time goes:
time: 22.9 us; the launch traced here: 22.7 us
  Pallas kernels  18.9 us (83%)
  local copies, waits for them, and re-layouts  3.16 us (14%)
  between operations  0.65 us (3%)
    pallas_call x1, Pallas kernels, per_device(): pl.pallas_call(functools.partial(kernel, tiles, groups, cols, D), out_sha...  18.9 us
    unnamed x4, local copies, waits for them, and re-layouts  3.16 us

commit v1 on v0

v1 whole, which is shorter than its diff:
```python
import functools
import math

import jax
import jax.numpy as jnp
from jax import lax
from jax.experimental import pallas as pl
from jax.experimental.pallas import tpu as pltpu
from jax.sharding import PartitionSpec as P

ITERS = 2
NS_STEPS = 6
LANES = 128
EPSILON = 1e-06
COUPLING = 0.5
FIELD = 0.3
F32 = jnp.float32
BF16 = jnp.bfloat16
MESH = pl.DeviceIdType.MESH


def iota(shape, axis):
    return lax.broadcasted_iota(jnp.int32, shape, axis)


def dot(a, b):
    return jnp.dot(a, b, preferred_element_type=F32)


def dot_nt(a, b):
    return lax.dot_general(a, b, (((1,), (1,)), ((), ())), preferred_element_type=F32)


def dot_tn(a, b):
    return lax.dot_general(a, b, (((0,), (0,)), ((), ())), preferred_element_type=F32)


def parts(value, count):
    out = []
    for _ in range(count):
        piece = value.astype(BF16)
        out.append(piece)
        value = value - piece.astype(F32)
    return out


def select_dot(value, selector, count):
    total = None
    for piece in parts(value, count):
        term = dot(piece, selector)
        total = term if total is None else total + term
    return total


def one_hot(mask):
    return jnp.where(mask, 1.0, 0.0).astype(BF16)


def build_kron(kron_ref, slot, first, second):
    D = first.shape[0]
    for d in range(D):
        kron_ref[slot, d * D : (d + 1) * D, :] = (first[d : d + 1, :] * second).astype(BF16)


def permutation(DD, rows, mixed, out_axis):
    p, k = iota((DD, DD), out_axis), iota((DD, DD), 1 - out_axis)
    row_bits = rows.bit_length() - 1
    return one_hot(k == (p & (rows - 1)) * mixed + (p >> row_bits))


def messages_kernel(tiles, groups, cols, D, a_ref, msg_ref, ax_ref, env_ref, mout_ref,
           x_ref, xt_ref, kron_ref, gram_ref,
           send_up, send_down, send_side, recv_up, recv_down, recv_side,
           send_sem, recv_sem):
    tile = lax.axis_index("tile")
    group = lax.axis_index("group")
    DD = D * D
    shift = D.bit_length() - 1
    halves = DD // LANES
    mixed = 2 * halves
    rows = DD // mixed
    legs = 4 * cols
    wide = legs * D
    has_up = tile > 0
    has_down = tile < tiles - 1

    barrier = pltpu.get_barrier_semaphore()

    @pl.when(has_up)
    def _():
        pl.semaphore_signal(barrier, inc=1, device_id={"tile": tile - 1}, device_id_type=MESH)

    @pl.when(has_down)
    def _():
        pl.semaphore_signal(barrier, inc=1, device_id={"tile": tile + 1}, device_id_type=MESH)

    pl.semaphore_signal(barrier, inc=1, device_id={"group": 1 - group}, device_id_type=MESH)

    lane = iota((D, DD), 1)
    row = iota((D, DD), 0)
    major = one_hot((lane >> shift) == row)
    minor = one_hot((lane & (D - 1)) == row)
    both = jnp.concatenate([major, minor], axis=1)
    major_t = one_hot((iota((DD, D), 0) >> shift) == iota((DD, D), 1))
    minor_t = one_hot((iota((DD, D), 0) & (D - 1)) == iota((DD, D), 1))

    unfold_mask = (lane >> shift) == row
    flat = msg_ref[...].reshape(legs, DD)
    spread = jnp.concatenate(
        [jnp.where(unfold_mask, flat[m : m + 1, :], 0.0) for m in range(legs)], axis=0
    )
    edge_all = select_dot(spread, minor_t, 3)
    edge = [edge_all[m * D : (m + 1) * D] for m in range(legs)]

    gather = permutation(DD, rows, mixed, 0)

    def unmix(i):
        for b in range(0, mixed, 2):
            pair = jnp.concatenate(
                [a_ref[i, b * DD : (b + 1) * DD, :], a_ref[i, (b + 1) * DD : (b + 2) * DD, :]],
                axis=1,
            )
            block = dot(gather, pair).astype(BF16)
            for c in range(2):
                for g in range(mixed):
                    x_ref[
                        i,
                        g % 2,
                        (b + c) * rows : (b + c + 1) * rows,
                        (g // 2) * LANES : (g // 2 + 1) * LANES,
                    ] = block[g * rows : (g + 1) * rows, c * LANES : (c + 1) * LANES]
        for s in range(2):
            xt_ref[i, s] = x_ref[i, s].T

    def reduce_major(gram, weight):
        total = gram[:D] * weight[0:1, :]
        for d in range(1, D):
            total = total + gram[d * D : (d + 1) * D] * weight[d : d + 1, :]
        return total

    def reduce_minor(gram, weight):
        return jnp.concatenate(
            [
                jnp.sum(gram[d * D : (d + 1) * D] * weight, axis=0, keepdims=True)
                for d in range(D)
            ],
            axis=0,
        )

    def kinds_of(totals):
        if len(totals) == 1:
            return totals
        return [totals[0] + totals[1], totals[0] - totals[1]]

    def outgoing(turn, incoming, last):
        stacked = jnp.concatenate([v.astype(BF16) for v in incoming], axis=0)
        spread = dot(stacked, both)
        kinds = 2 if last else 1

        def by_major(m):
            return spread[m * D : (m + 1) * D, :DD]

        def by_minor(m):
            return spread[m * D : (m + 1) * D, DD:]

        def normalised(totals, selector, slots):
            blocks = []
            for kind in range(kinds):
                rows_of = jnp.concatenate([t[kind] for t in totals], axis=0)
                blocks.append(select_dot(rows_of, selector, 2))
            out = {}
            for n, slot in enumerate(slots):
                own = [b[n * D : (n + 1) * D] for b in blocks]
                power = jnp.sum(own[0] * own[0], axis=(0, 1), keepdims=True) / DD
                scale = jnp.sqrt(power + EPSILON)
                out[slot] = [v / scale for v in own]
            return out

        firsts = []
        for i in range(cols):
            if turn == 0:
                unmix(i)
            for path in range(2):
                left, right = (x_ref, xt_ref) if path == 0 else (xt_ref, x_ref)
                far = i * 4 + 2 * (1 - path)
                near = i * 4 + 2 * path
                slot = i * 2 + path
                build_kron(kron_ref, slot, by_major(far), by_minor(far + 1))
                y = [dot(left[i, s], kron_ref[slot]).astype(BF16) for s in range(2)]
                if last:
                    grams = [dot(y[s], right[i, s]) for s in range(2)]
                else:
                    grams = [dot(y[0], right[i, 0]) + dot(y[1], right[i, 1])]
                for k, gram in enumerate(grams):
                    gram_ref[slot, k] = gram
                firsts.append(kinds_of([reduce_minor(g, by_minor(near + 1)) for g in grams]))

        def seconds(slots):
            totals = []
            for slot in slots:
                weight = by_major((slot // 2) * 4 + 2 * (slot % 2))
                totals.append(
                    kinds_of([reduce_major(gram_ref[slot, k], weight) for k in range(kinds)])
                )
            return normalised(totals, minor_t, slots)

        vertical = normalised(firsts, major_t, list(range(2 * cols)))
        ends = [0, 2 * cols - 1]
        sides = seconds(ends)

        def rest():
            others = [slot for slot in range(2 * cols) if slot not in ends]
            if others:
                sides.update(seconds(others))
            values = []
            for kind in range(kinds):
                blocks = []
                for slot in range(2 * cols):
                    blocks += [vertical[slot][kind], sides[slot][kind]]
                values.append(blocks)
            return values

        return vertical, sides, rest

    def exchange(turn, vertical, sides, kinds):
        width = kinds * cols * D

        def packed(path):
            return jnp.concatenate(
                [vertical[2 * i + path][k] for k in range(kinds) for i in range(cols)], axis=1
            )

        up_src = send_up.at[turn]
        down_src = send_down.at[turn]
        side_src = send_side.at[turn]
        send_up[turn, :, :width] = packed(0)
        send_down[turn, :, :width] = packed(1)
        side_right = jnp.concatenate(sides[2 * cols - 1], axis=1)
        side_left = jnp.concatenate(sides[0], axis=1)
        send_side[turn, :, : kinds * D] = jnp.where(group == 0, side_right, side_left)

        def copy(src, dst, k, device):
            return pltpu.make_async_remote_copy(
                src_ref=src, dst_ref=dst.at[turn], send_sem=send_sem.at[turn, k],
                recv_sem=recv_sem.at[turn, k], device_id=device, device_id_type=MESH,
            )

        to_up = copy(up_src, recv_down, 0, {"tile": tile - 1})
        to_down = copy(down_src, recv_up, 1, {"tile": tile + 1})
        to_side = copy(side_src, recv_side, 2, {"group": 1 - group})

        @pl.when(has_up)
        def _():
            to_up.start()

        @pl.when(has_down)
        def _():
            to_down.start()

        to_side.start()
        return to_up, to_down, to_side

    def finish(turn, copies, values):
        to_up, to_down, to_side = copies
        kinds = len(values)
        width = kinds * cols * D

        def border(leg):
            blocks = [edge[i * 4 + leg] for i in range(cols)]
            if kinds == 2:
                blocks += [jnp.zeros((D, D), F32)] * cols
            return jnp.concatenate(blocks, axis=1)

        @pl.when(has_up)
        def _():
            to_up.wait_send()
            to_down.wait_recv()

        @pl.when(jnp.logical_not(has_up))
        def _():
            recv_up[turn, :, :width] = border(0)

        @pl.when(has_down)
        def _():
            to_down.wait_send()
            to_up.wait_recv()

        @pl.when(jnp.logical_not(has_down))
        def _():
            recv_down[turn, :, :width] = border(2)

        to_side.wait()
        from_up, from_down, from_side = recv_up[turn], recv_down[turn], recv_side[turn]
        routed = []
        for kind in range(kinds):
            blocks = []
            for i in range(cols):
                at = (kind * cols + i) * D
                side = from_side[:, kind * D : (kind + 1) * D]
                zero = jnp.zeros((D, D), F32)
                out_left = edge[i * 4 + 1] if kind == 0 else zero
                out_right = edge[i * 4 + 3] if kind == 0 else zero
                blocks.append(from_up[:, at : at + D])
                if i > 0:
                    blocks.append(values[kind][(i - 1) * 4 + 3])
                else:
                    blocks.append(jnp.where(group == 0, out_left, side))
                blocks.append(from_down[:, at : at + D])
                if i < cols - 1:
                    blocks.append(values[kind][(i + 1) * 4 + 1])
                else:
                    blocks.append(jnp.where(group == groups - 1, out_right, side))
            routed.append(blocks)
        return routed

    incoming = edge
    for turn in range(ITERS):
        last = turn == ITERS - 1
        vertical, sides, rest = outgoing(turn, incoming, last)
        if turn == 0:
            inside = jnp.logical_and(has_up, has_down)

            @pl.when(inside)
            def _():
                pl.semaphore_wait(barrier, 3)

            @pl.when(jnp.logical_not(inside))
            def _():
                pl.semaphore_wait(barrier, 2)

        copies = exchange(turn, vertical, sides, 2 if last else 1)
        values = rest()
        if turn == 0:
            for i in range(cols):
                a0, a1 = x_ref[i, 0].astype(F32), x_ref[i, 1].astype(F32)
                ch, sh = math.cosh(FIELD), math.sinh(FIELD)
                ax_ref[i, 0] = (ch * a0 + sh * a1).astype(BF16)
                ax_ref[i, 1] = (ch * a1 + sh * a0).astype(BF16)
        routed = finish(turn, copies, values)
        incoming = routed[0]

    mout_ref[...] = jnp.concatenate(incoming, axis=0)
    env_ref[0] = jnp.concatenate([o + n for o, n in zip(values[0], routed[0])], axis=1)
    env_ref[1] = jnp.concatenate([o + n for o, n in zip(values[1], routed[1])], axis=1)
    lane_w = iota((D, wide), 1)
    leg_of = (lane_w >> shift) & 3
    col_of = (lane_w >> (shift + 2)) + group * cols
    at_edge = (
        ((leg_of == 0) & (tile == 0))
        | ((leg_of == 2) & (tile == tiles - 1))
        | ((leg_of == 1) & (col_of == 0))
        | ((leg_of == 3) & (col_of == groups * cols - 1))
    )
    env_ref[2] = jnp.where(at_edge, 1.0, 0.0).astype(F32)


def gates_kernel(cols, D, ax_ref, env_ref, in_ref, out_hbm, mout_ref,
                 kron_ref, out_ref, store_sem):
    DD = D * D
    shift = D.bit_length() - 1
    mixed = 2 * (DD // LANES)
    rows = DD // mixed
    legs = 4 * cols
    wide = legs * D
    lane = iota((D, DD), 1)
    row = iota((D, DD), 0)
    major = one_hot((lane >> shift) == row)
    minor = one_hot((lane & (D - 1)) == row)
    both = jnp.concatenate([major, minor], axis=1)

    spread = select_dot(in_ref[...], minor, 3)
    unfold_mask = (lane >> shift) == row
    flat_rows = [
        jnp.sum(
            jnp.where(unfold_mask, spread[m * D : (m + 1) * D], 0.0), axis=0, keepdims=True
        )
        for m in range(legs)
    ]
    mout_ref[...] = jnp.concatenate(flat_rows, axis=0).reshape(cols, 4, DD)

    g0, g1 = math.cosh(COUPLING), math.sinh(COUPLING)
    cross = math.sqrt(g0 * g1)
    root2 = math.sqrt(2.0)
    msg_sum, twist_sum = env_ref[0], env_ref[1]
    y_top = ((g0 * msg_sum + cross * twist_sum) / root2).astype(BF16)
    y_bot = ((cross * twist_sum + g1 * msg_sum) / root2).astype(BF16)
    y_both = jnp.concatenate([y_top, y_bot], axis=0)
    same = (iota((wide, wide), 0) >> shift) == (iota((wide, wide), 1) >> shift)
    same_bf = one_hot(same)
    lane_w = iota((D, wide), 1)
    unit = jnp.where((lane_w & (D - 1)) == iota((D, wide), 0), 1.0, 0.0).astype(F32)

    def diagonal(value):
        return jnp.concatenate([value] * legs, axis=0) * same_bf

    def times(left, right):
        count = left.shape[0]
        (l_hi, l_lo), (r_hi, r_lo) = parts(left, 2), parts(right, 2)
        main = dot(jnp.concatenate([l_hi, l_lo], axis=0), diagonal(r_hi))
        return main[:count] + (main[count:] + dot(l_hi, diagonal(r_lo)))

    full = jnp.where(same, dot_tn(y_both, y_both), 0.0)
    gram = full[:D]
    for m in range(1, legs):
        gram = gram + full[m * D : (m + 1) * D]
    diag = jnp.sum(gram * unit, axis=0, keepdims=True)
    trace = select_dot(jnp.broadcast_to(diag, (8, wide)), same_bf, 3)[0:1] + EPSILON
    current = gram / trace
    factor = 1.5 * unit - 0.5 * current
    inverse = factor
    current = times(current, factor)
    for step in range(1, NS_STEPS):
        factor = 1.5 * unit - 0.5 * times(inverse, current)
        if step < NS_STEPS - 1:
            stepped = times(jnp.concatenate([inverse, current], axis=0), factor)
            inverse, current = stepped[:D], stepped[D:]
        else:
            inverse = times(inverse, factor)
    q_both = dot(y_both, diagonal(inverse.astype(BF16))) / jnp.sqrt(trace)
    first = math.sqrt(g0) * q_both[:D]
    second = math.sqrt(g1) * q_both[D:]
    at_edge = env_ref[2] > 0.5
    scatter = permutation(DD, rows, mixed, 1)
    spreads = []
    for weight in (first + second, first - second):
        weight = jnp.where(at_edge, unit, weight)
        spreads.append(dot(weight.T.astype(BF16), both))
    stores = [
        pltpu.make_async_copy(out_ref.at[i], out_hbm.at[i], store_sem.at[i]) for i in range(cols)
    ]
    pairs = []
    for i in range(cols):
        m = i * 4
        gated = []
        for s in range(2):
            w = spreads[s]
            slot = (i * 2 + s) * 2
            build_kron(
                kron_ref, slot, w[(m + 2) * D : (m + 3) * D, :DD], w[(m + 3) * D : (m + 4) * D, DD:]
            )
            build_kron(
                kron_ref, slot + 1, w[m * D : (m + 1) * D, :DD], w[(m + 1) * D : (m + 2) * D, DD:]
            )
            half = dot_nt(ax_ref[i, s], kron_ref[slot]).astype(BF16)
            gated.append(dot(kron_ref[slot + 1], half).astype(BF16))
        pairs.append(gated)
    for i, gated in enumerate(pairs):
        for b in range(0, mixed, 2):
            block = jnp.concatenate(
                [
                    jnp.concatenate(
                        [
                            gated[g % 2][
                                (b + c) * rows : (b + c + 1) * rows,
                                (g // 2) * LANES : (g // 2 + 1) * LANES,
                            ]
                            for c in range(2)
                        ],
                        axis=1,
                    )
                    for g in range(mixed)
                ],
                axis=0,
            )
            done = dot(scatter, block).astype(BF16)
            for c in range(2):
                out_ref[i, (b + c) * DD : (b + c + 1) * DD, :] = done[
                    :, c * LANES : (c + 1) * LANES
                ]
        stores[i].start()
    for store in stores:
        store.wait()


def per_device(tiles, groups, site_tensors, msg_in):
    _, cols, _, size = site_tensors.shape
    DD = msg_in.shape[-1]
    D = math.isqrt(DD)
    chunks = size // LANES
    a = site_tensors.reshape(cols, 2, chunks, LANES).transpose(0, 2, 1, 3)
    a = a.reshape(cols, 2 * chunks, LANES)
    wide = 2 * cols * D
    legs = 4 * cols
    vmem = pl.BlockSpec(memory_space=pltpu.VMEM)
    anywhere = pl.BlockSpec(memory_space=pl.ANY)
    gated, env, stacked = pl.pallas_call(
        functools.partial(messages_kernel, tiles, groups, cols, D),
        out_shape=(
            jax.ShapeDtypeStruct((cols, 2, DD, DD), BF16),
            jax.ShapeDtypeStruct((3, D, legs * D), F32),
            jax.ShapeDtypeStruct((legs * D, D), F32),
        ),
        in_specs=[vmem, vmem],
        out_specs=(vmem, vmem, vmem),
        scratch_shapes=[
            pltpu.VMEM((cols, 2, DD, DD), BF16),
            pltpu.VMEM((cols, 2, DD, DD), BF16),
            pltpu.VMEM((2 * cols, DD, DD), BF16),
            pltpu.VMEM((2 * cols, 2, DD, DD), F32),
            pltpu.VMEM((ITERS, D, wide), F32),
            pltpu.VMEM((ITERS, D, wide), F32),
            pltpu.VMEM((ITERS, D, 2 * D), F32),
            pltpu.VMEM((ITERS, D, wide), F32),
            pltpu.VMEM((ITERS, D, wide), F32),
            pltpu.VMEM((ITERS, D, 2 * D), F32),
            pltpu.SemaphoreType.DMA((ITERS, 3)),
            pltpu.SemaphoreType.DMA((ITERS, 3)),
        ],
        compiler_params=pltpu.CompilerParams(
            collective_id=0, has_side_effects=True, vmem_limit_bytes=24 * 2**20
        ),
    )(a, msg_in[0])
    out, messages = pl.pallas_call(
        functools.partial(gates_kernel, cols, D),
        out_shape=(
            jax.ShapeDtypeStruct(a.shape, BF16),
            jax.ShapeDtypeStruct((cols, 4, DD), F32),
        ),
        in_specs=[vmem, vmem, vmem],
        out_specs=(anywhere, vmem),
        scratch_shapes=[
            pltpu.VMEM((4 * cols, DD, DD), BF16),
            pltpu.VMEM(a.shape, BF16),
            pltpu.SemaphoreType.DMA((cols,)),
        ],
        compiler_params=pltpu.CompilerParams(vmem_limit_bytes=24 * 2**20),
    )(gated, env, stacked)
    out = out.reshape(cols, chunks, 2, LANES).transpose(0, 2, 1, 3)
    return out.reshape(1, cols, 2, size), messages[None]


def solution(mesh):
    spec = P("tile", "group", None, None)
    return jax.shard_map(
        functools.partial(per_device, mesh.shape["tile"], mesh.shape["group"]),
        mesh=mesh, in_specs=(spec, spec), out_specs=(spec, spec), check_vma=False,
    )
```

time: 22.9 us -> 19.7 us (0.86)
  Pallas kernels: 18.9 us -> 16.9 us
  local copies, waits for them, and re-layouts: 3.16 us -> 1.83 us
    pallas_call x1 -> x2, Pallas kernels: 18.9 us -> 16.9 us  [the longest x1 11.7 us: per_device(): pl.pallas_call(functools.partial(messages_kernel, tiles, groups, cols, D)...]
    unnamed x4, local copies, waits for them, and re-layouts: 3.16 us -> 1.83 us
where the time goes in v1:
time: 19.7 us; the launch traced here: 19.4 us
  Pallas kernels  16.9 us (86%)
  local copies, waits for them, and re-layouts  1.83 us (9%)
  between operations  0.65 us (3%)
    pallas_call x1, Pallas kernels, per_device(): pl.pallas_call(functools.partial(messages_kernel, tiles, groups, cols, D)...  11.7 us
    pallas_call x1, Pallas kernels, per_device(): pl.pallas_call(functools.partial(gates_kernel, cols, D), out_shape=(jax.S...  5.24 us
    unnamed x4, local copies, waits for them, and re-layouts  1.83 us

profile of v1, /device:TPU:1, one launch (start us, length us, event | category | flops | bytes accessed | tf_op | source)
XLA Modules:
  0.0 19.4 jit_solution(11853042523620836249)
XLA Ops:
  0.6 0.0 copy-start
  0.6 1.1 %copy-done = bf16[1,3,2,65536]{3,2,1,0:T(2,128)(2,1)S(1)} copy-done((bf16[1,3,2,65536]{3,2,1,0:T(2,128)(2,1)S(1)}, bf16[1,3,2,65536]{3,2,1,0:T(2,128)(2,1)}, u32[]{:S(2)}) %copy-start) | copy-done | bytes 786456
  1.8 0.0 copy-start.1
  1.8 0.7 %copy-done.1 = f32[1,3,4,256]{3,2,1,0:T(4,128)S(1)} copy-done((f32[1,3,4,256]{3,2,1,0:T(4,128)S(1)}, f32[1,3,4,256]{3,2,1,0:T(4,128)}, u32[]{:S(2)}) %copy-start.1) | copy-done | bytes 12312
  2.5 11.7 %shard_map.41 = (bf16[3,2,256,256]{3,2,1,0:T(8,128)(2,1)S(1)}, f32[3,16,192]{2,1,0:T(8,128)S(1)}, f32[192,16]{1,0:T(8,128)S(1)}) custom-call(bf16[3,1024,128]{2,1,0:T(8,128)(2,1)S(1)} %bitcast.12, f32[3,4,256]{2,1,0:T(4,128)S(1)} %bitcast.13), custom_call_target="tpu_custom_call" | custom-call | tf_op jit(solution)/shard_map/pallas_call | solution.py:486
  14.2 5.2 %shard_map.42 = (bf16[3,1024,128]{2,1,0:T(8,128)(2,1)}, f32[3,4,256]{2,1,0:T(4,128)}) custom-call(bf16[3,2,256,256]{3,2,1,0:T(8,128)(2,1)S(1)} %get-tuple-element.7.ax_ref, f32[3,16,192]{2,1,0:T(8,128)S(1)} %get-tuple-element.8.env_ref, f32[192,16]{1,0:T(8,128)S(1)} %get-tuple-element.9.in_ref), custom_call_target="tpu_custom_call" | custom-call | tf_op jit(solution)/shard_map/pallas_call | solution.py:513
Async XLA Ops:
  0.6 1.1 %copy-start = (bf16[1,3,2,65536]{3,2,1,0:T(2,128)(2,1)S(1)}, bf16[1,3,2,65536]{3,2,1,0:T(2,128)(2,1)}, u32[]{:S(2)}) copy-start(bf16[1,3,2,65536]{3,2,1,0:T(2,128)(2,1)} %param.2) | copy-start | bytes 2359300
  1.8 0.7 %copy-start.1 = (f32[1,3,4,256]{3,2,1,0:T(4,128)S(1)}, f32[1,3,4,256]{3,2,1,0:T(4,128)}, u32[]{:S(2)}) copy-start(f32[1,3,4,256]{3,2,1,0:T(4,128)} %param.3) | copy-start | bytes 36868

commit v2 on v1

--- a/solution.py
+++ b/solution.py
@@ -354,8 +354,8 @@
     env_ref[2] = jnp.where(at_edge, 1.0, 0.0).astype(F32)
 
 
-def gates_kernel(cols, D, ax_ref, env_ref, in_ref, out_hbm, mout_ref,
-                 kron_ref, out_ref, store_sem):
+def gates_kernel(cols, D, ax_ref, env_ref, in_ref, out_hbm, mout_hbm,
+                 kron_ref, out_ref, mout_ref, store_sem):
     DD = D * D
     shift = D.bit_length() - 1
     mixed = 2 * (DD // LANES)
@@ -377,6 +377,8 @@
         for m in range(legs)
     ]
     mout_ref[...] = jnp.concatenate(flat_rows, axis=0).reshape(cols, 4, DD)
+    store_msg = pltpu.make_async_copy(mout_ref, mout_hbm, store_sem.at[cols])
+    store_msg.start()
 
     g0, g1 = math.cosh(COUPLING), math.sinh(COUPLING)
     cross = math.sqrt(g0 * g1)
@@ -428,8 +430,7 @@
     stores = [
         pltpu.make_async_copy(out_ref.at[i], out_hbm.at[i], store_sem.at[i]) for i in range(cols)
     ]
-    pairs = []
-    for i in range(cols):
+    def gate(i):
         m = i * 4
         gated = []
         for s in range(2):
@@ -443,8 +444,9 @@
             )
             half = dot_nt(ax_ref[i, s], kron_ref[slot]).astype(BF16)
             gated.append(dot(kron_ref[slot + 1], half).astype(BF16))
-        pairs.append(gated)
-    for i, gated in enumerate(pairs):
+        return gated
+
+    def emit(i, gated):
         for b in range(0, mixed, 2):
             block = jnp.concatenate(
                 [
@@ -468,7 +470,13 @@
                     :, c * LANES : (c + 1) * LANES
                 ]
         stores[i].start()
-    for store in stores:
+
+    waiting = gate(0)
+    for i in range(cols):
+        following = gate(i + 1) if i + 1 < cols else None
+        emit(i, waiting)
+        waiting = following
+    for store in stores + [store_msg]:
         store.wait()
 
 
@@ -482,7 +490,7 @@
     wide = 2 * cols * D
     legs = 4 * cols
     vmem = pl.BlockSpec(memory_space=pltpu.VMEM)
-    anywhere = pl.BlockSpec(memory_space=pl.ANY)
+    hbm = pl.BlockSpec(memory_space=pltpu.HBM)
     gated, env, stacked = pl.pallas_call(
         functools.partial(messages_kernel, tiles, groups, cols, D),
         out_shape=(
@@ -517,11 +525,12 @@
             jax.ShapeDtypeStruct((cols, 4, DD), F32),
         ),
         in_specs=[vmem, vmem, vmem],
-        out_specs=(anywhere, vmem),
+        out_specs=(hbm, hbm),
         scratch_shapes=[
             pltpu.VMEM((4 * cols, DD, DD), BF16),
             pltpu.VMEM(a.shape, BF16),
-            pltpu.SemaphoreType.DMA((cols,)),
+            pltpu.VMEM((cols, 4, DD), F32),
+            pltpu.SemaphoreType.DMA((cols + 1,)),
         ],
         compiler_params=pltpu.CompilerParams(vmem_limit_bytes=24 * 2**20),
     )(gated, env, stacked)

time: 19.7 us -> 19.3 us (0.980)
  Pallas kernels: 16.9 us -> 16.5 us
    pallas_call x1, Pallas kernels: 5.24 us -> 4.83 us  [per_device(): pl.pallas_call(functools.partial(gates_kernel, cols, D), out_shape=(jax.S...]
where the time goes in v2:
time: 19.3 us; the launch traced here: 19 us
  Pallas kernels  16.5 us (85%)
  local copies, waits for them, and re-layouts  1.83 us (9%)
  between operations  0.65 us (3%)
    pallas_call x1, Pallas kernels, per_device(): pl.pallas_call(functools.partial(messages_kernel, tiles, groups, cols, D)...  11.7 us
    pallas_call x1, Pallas kernels, per_device(): pl.pallas_call(functools.partial(gates_kernel, cols, D), out_shape=(jax.S...  4.83 us
    unnamed x4, local copies, waits for them, and re-layouts  1.83 us

profile of v2, /device:TPU:1, one launch (start us, length us, event | category | flops | bytes accessed | tf_op | source)
XLA Modules:
  0.0 19.0 jit_solution(16019051047325696535)
XLA Ops:
  0.6 0.0 copy-start
  0.6 1.1 %copy-done = bf16[1,3,2,65536]{3,2,1,0:T(2,128)(2,1)S(1)} copy-done((bf16[1,3,2,65536]{3,2,1,0:T(2,128)(2,1)S(1)}, bf16[1,3,2,65536]{3,2,1,0:T(2,128)(2,1)}, u32[]{:S(2)}) %copy-start) | copy-done | bytes 786456
  1.8 0.0 copy-start.1
  1.8 0.7 %copy-done.1 = f32[1,3,4,256]{3,2,1,0:T(4,128)S(1)} copy-done((f32[1,3,4,256]{3,2,1,0:T(4,128)S(1)}, f32[1,3,4,256]{3,2,1,0:T(4,128)}, u32[]{:S(2)}) %copy-start.1) | copy-done | bytes 12312
  2.5 11.7 %shard_map.41 = (bf16[3,2,256,256]{3,2,1,0:T(8,128)(2,1)S(1)}, f32[3,16,192]{2,1,0:T(8,128)S(1)}, f32[192,16]{1,0:T(8,128)S(1)}) custom-call(bf16[3,1024,128]{2,1,0:T(8,128)(2,1)S(1)} %bitcast.12, f32[3,4,256]{2,1,0:T(4,128)S(1)} %bitcast.13), custom_call_target="tpu_custom_call" | custom-call | tf_op jit(solution)/shard_map/pallas_call | solution.py:494
  14.2 4.8 %shard_map.42 = (bf16[3,1024,128]{2,1,0:T(8,128)(2,1)}, f32[3,4,256]{2,1,0:T(4,128)}) custom-call(bf16[3,2,256,256]{3,2,1,0:T(8,128)(2,1)S(1)} %get-tuple-element.7.ax_ref, f32[3,16,192]{2,1,0:T(8,128)S(1)} %get-tuple-element.8.env_ref, f32[192,16]{1,0:T(8,128)S(1)} %get-tuple-element.9.in_ref), custom_call_target="tpu_custom_call" | custom-call | tf_op jit(solution)/shard_map/pallas_call | solution.py:521
Async XLA Ops:
  0.6 1.1 %copy-start = (bf16[1,3,2,65536]{3,2,1,0:T(2,128)(2,1)S(1)}, bf16[1,3,2,65536]{3,2,1,0:T(2,128)(2,1)}, u32[]{:S(2)}) copy-start(bf16[1,3,2,65536]{3,2,1,0:T(2,128)(2,1)} %param.2) | copy-start | bytes 2359300
  1.8 0.7 %copy-start.1 = (f32[1,3,4,256]{3,2,1,0:T(4,128)S(1)}, f32[1,3,4,256]{3,2,1,0:T(4,128)}, u32[]{:S(2)}) copy-start(f32[1,3,4,256]{3,2,1,0:T(4,128)} %param.3) | copy-start | bytes 36868

commit v3 on v2

--- a/solution.py
+++ b/solution.py
@@ -69,8 +69,8 @@
 
 
 def messages_kernel(tiles, groups, cols, D, a_ref, msg_ref, ax_ref, env_ref, mout_ref,
-           x_ref, xt_ref, kron_ref, gram_ref,
-           send_up, send_down, send_side, recv_up, recv_down, recv_side,
+           xx_ref, kron_ref, gram_ref,
+           send_vert, send_side, recv_vert, recv_side,
            send_sem, recv_sem):
     tile = lax.axis_index("tile")
     group = lax.axis_index("group")
@@ -83,6 +83,8 @@
     wide = legs * D
     has_up = tile > 0
     has_down = tile < tiles - 1
+    flip = tile % 2
+    x_ref, xt_ref = xx_ref.at[0], xx_ref.at[1]
 
     barrier = pltpu.get_barrier_semaphore()
 
@@ -176,37 +178,55 @@
                 out[slot] = [v / scale for v in own]
             return out
 
-        firsts = []
-        for i in range(cols):
-            if turn == 0:
-                unmix(i)
-            for path in range(2):
-                left, right = (x_ref, xt_ref) if path == 0 else (xt_ref, x_ref)
-                far = i * 4 + 2 * (1 - path)
-                near = i * 4 + 2 * path
-                slot = i * 2 + path
-                build_kron(kron_ref, slot, by_major(far), by_minor(far + 1))
-                y = [dot(left[i, s], kron_ref[slot]).astype(BF16) for s in range(2)]
-                if last:
-                    grams = [dot(y[s], right[i, s]) for s in range(2)]
-                else:
-                    grams = [dot(y[0], right[i, 0]) + dot(y[1], right[i, 1])]
-                for k, gram in enumerate(grams):
-                    gram_ref[slot, k] = gram
-                firsts.append(kinds_of([reduce_minor(g, by_minor(near + 1)) for g in grams]))
-
         def seconds(slots):
             totals = []
             for slot in slots:
-                weight = by_major((slot // 2) * 4 + 2 * (slot % 2))
+                i, path = slot // 2, slot % 2
+                held = i * 2 + (path + flip) % 2
+                weight = by_major(i * 4 + 2 * path)
                 totals.append(
-                    kinds_of([reduce_major(gram_ref[slot, k], weight) for k in range(kinds)])
+                    kinds_of([reduce_major(gram_ref[held, k], weight) for k in range(kinds)])
                 )
             return normalised(totals, minor_t, slots)
 
-        vertical = normalised(firsts, major_t, list(range(2 * cols)))
+        phases, copies = [], []
+        if turn == 0:
+            for i in range(cols):
+                unmix(i)
+        for phase in range(2):
+            path = (phase + flip) % 2
+            upward = flip == phase
+            firsts = []
+            for i in range(cols):
+                m = i * 4
+                far_a = jnp.where(upward, by_major(m + 2), by_major(m))
+                far_b = jnp.where(upward, by_minor(m + 3), by_minor(m + 1))
+                near_b = jnp.where(upward, by_minor(m + 1), by_minor(m + 3))
+                slot = i * 2 + phase
+                build_kron(kron_ref, slot, far_a, far_b)
+                y = [dot(xx_ref[path, i, s], kron_ref[slot]).astype(BF16) for s in range(2)]
+                if last:
+                    grams = [dot(y[s], xx_ref[1 - path, i, s]) for s in range(2)]
+                else:
+                    grams = [dot(y[0], xx_ref[1 - path, i, 0]) + dot(y[1], xx_ref[1 - path, i, 1])]
+                for k, gram in enumerate(grams):
+                    gram_ref[slot, k] = gram
+                firsts.append(kinds_of([reduce_minor(g, near_b) for g in grams]))
+            done = normalised(firsts, major_t, list(range(cols)))
+            phases.append(done)
+            if turn == 0 and phase == 0:
+                enter()
+            copies.append(send_vertical(turn, phase, done, kinds))
+
         ends = [0, 2 * cols - 1]
         sides = seconds(ends)
+        vertical = {}
+        for i in range(cols):
+            for path in range(2):
+                vertical[2 * i + path] = [
+                    jnp.where(flip == 0, u, v)
+                    for u, v in zip(phases[path][i], phases[1 - path][i])
+                ]
 
         def rest():
             others = [slot for slot in range(2 * cols) if slot not in ends]
@@ -220,48 +240,53 @@
                 values.append(blocks)
             return values
 
-        return vertical, sides, rest
-
-    def exchange(turn, vertical, sides, kinds):
-        width = kinds * cols * D
-
-        def packed(path):
-            return jnp.concatenate(
-                [vertical[2 * i + path][k] for k in range(kinds) for i in range(cols)], axis=1
-            )
-
-        up_src = send_up.at[turn]
-        down_src = send_down.at[turn]
-        side_src = send_side.at[turn]
-        send_up[turn, :, :width] = packed(0)
-        send_down[turn, :, :width] = packed(1)
+        return copies, sides, rest
+
+    def enter():
+        inside = jnp.logical_and(has_up, has_down)
+
+        @pl.when(inside)
+        def _():
+            pl.semaphore_wait(barrier, 3)
+
+        @pl.when(jnp.logical_not(inside))
+        def _():
+            pl.semaphore_wait(barrier, 2)
+
+    def vertical_copy(turn, phase, slot, target):
+        return pltpu.make_async_remote_copy(
+            src_ref=send_vert.at[turn, phase], dst_ref=recv_vert.at[turn, slot],
+            send_sem=send_sem.at[turn, phase], recv_sem=recv_sem.at[turn, slot],
+            device_id={"tile": target}, device_id_type=MESH,
+        )
+
+    def send_vertical(turn, phase, done, kinds):
+        send_vert[turn, phase, :, : kinds * cols * D] = jnp.concatenate(
+            [done[i][k] for k in range(kinds) for i in range(cols)], axis=1
+        )
+        path = (phase + flip) % 2
+        exists = jnp.where(flip == phase, tile, tiles - 1 - tile) > 0
+        copy = vertical_copy(turn, phase, 1 - path, tile - 1 + 2 * path)
+
+        @pl.when(exists)
+        def _():
+            copy.start()
+
+        return copy, exists
+
+    def exchange(turn, sides, kinds):
         side_right = jnp.concatenate(sides[2 * cols - 1], axis=1)
         side_left = jnp.concatenate(sides[0], axis=1)
         send_side[turn, :, : kinds * D] = jnp.where(group == 0, side_right, side_left)
-
-        def copy(src, dst, k, device):
-            return pltpu.make_async_remote_copy(
-                src_ref=src, dst_ref=dst.at[turn], send_sem=send_sem.at[turn, k],
-                recv_sem=recv_sem.at[turn, k], device_id=device, device_id_type=MESH,
-            )
-
-        to_up = copy(up_src, recv_down, 0, {"tile": tile - 1})
-        to_down = copy(down_src, recv_up, 1, {"tile": tile + 1})
-        to_side = copy(side_src, recv_side, 2, {"group": 1 - group})
-
-        @pl.when(has_up)
-        def _():
-            to_up.start()
-
-        @pl.when(has_down)
-        def _():
-            to_down.start()
-
+        to_side = pltpu.make_async_remote_copy(
+            src_ref=send_side.at[turn], dst_ref=recv_side.at[turn],
+            send_sem=send_sem.at[turn, 2], recv_sem=recv_sem.at[turn, 2],
+            device_id={"group": 1 - group}, device_id_type=MESH,
+        )
         to_side.start()
-        return to_up, to_down, to_side
-
-    def finish(turn, copies, values):
-        to_up, to_down, to_side = copies
+        return to_side
+
+    def finish(turn, copies, to_side, values):
         kinds = len(values)
         width = kinds * cols * D
 
@@ -271,26 +296,24 @@
                 blocks += [jnp.zeros((D, D), F32)] * cols
             return jnp.concatenate(blocks, axis=1)
 
-        @pl.when(has_up)
-        def _():
-            to_up.wait_send()
-            to_down.wait_recv()
-
-        @pl.when(jnp.logical_not(has_up))
-        def _():
-            recv_up[turn, :, :width] = border(0)
-
-        @pl.when(has_down)
-        def _():
-            to_down.wait_send()
-            to_up.wait_recv()
-
-        @pl.when(jnp.logical_not(has_down))
-        def _():
-            recv_down[turn, :, :width] = border(2)
+        for copy, exists in copies:
+            @pl.when(exists)
+            def _():
+                copy.wait_send()
+
+        for slot, present, leg, target in (
+            (0, has_up, 0, tile - 1), (1, has_down, 2, tile + 1)
+        ):
+            @pl.when(present)
+            def _():
+                vertical_copy(turn, 0, slot, target).wait_recv()
+
+            @pl.when(jnp.logical_not(present))
+            def _():
+                recv_vert[turn, slot, :, :width] = border(leg)
 
         to_side.wait()
-        from_up, from_down, from_side = recv_up[turn], recv_down[turn], recv_side[turn]
+        from_up, from_down, from_side = recv_vert[turn, 0], recv_vert[turn, 1], recv_side[turn]
         routed = []
         for kind in range(kinds):
             blocks = []
@@ -316,19 +339,8 @@
     incoming = edge
     for turn in range(ITERS):
         last = turn == ITERS - 1
-        vertical, sides, rest = outgoing(turn, incoming, last)
-        if turn == 0:
-            inside = jnp.logical_and(has_up, has_down)
-
-            @pl.when(inside)
-            def _():
-                pl.semaphore_wait(barrier, 3)
-
-            @pl.when(jnp.logical_not(inside))
-            def _():
-                pl.semaphore_wait(barrier, 2)
-
-        copies = exchange(turn, vertical, sides, 2 if last else 1)
+        copies, sides, rest = outgoing(turn, incoming, last)
+        to_side = exchange(turn, sides, 2 if last else 1)
         values = rest()
         if turn == 0:
             for i in range(cols):
@@ -336,7 +348,7 @@
                 ch, sh = math.cosh(FIELD), math.sinh(FIELD)
                 ax_ref[i, 0] = (ch * a0 + sh * a1).astype(BF16)
                 ax_ref[i, 1] = (ch * a1 + sh * a0).astype(BF16)
-        routed = finish(turn, copies, values)
+        routed = finish(turn, copies, to_side, values)
         incoming = routed[0]
 
     mout_ref[...] = jnp.concatenate(incoming, axis=0)
@@ -501,15 +513,12 @@
         in_specs=[vmem, vmem],
         out_specs=(vmem, vmem, vmem),
         scratch_shapes=[
-            pltpu.VMEM((cols, 2, DD, DD), BF16),
-            pltpu.VMEM((cols, 2, DD, DD), BF16),
+            pltpu.VMEM((2, cols, 2, DD, DD), BF16),
             pltpu.VMEM((2 * cols, DD, DD), BF16),
             pltpu.VMEM((2 * cols, 2, DD, DD), F32),
-            pltpu.VMEM((ITERS, D, wide), F32),
-            pltpu.VMEM((ITERS, D, wide), F32),
+            pltpu.VMEM((ITERS, 2, D, wide), F32),
             pltpu.VMEM((ITERS, D, 2 * D), F32),
-            pltpu.VMEM((ITERS, D, wide), F32),
-            pltpu.VMEM((ITERS, D, wide), F32),
+            pltpu.VMEM((ITERS, 2, D, wide), F32),
             pltpu.VMEM((ITERS, D, 2 * D), F32),
             pltpu.SemaphoreType.DMA((ITERS, 3)),
             pltpu.SemaphoreType.DMA((ITERS, 3)),

time: 19.3 us -> 20.4 us (1.057)
  the two profiles are of different devices: /device:TPU:1 before, /device:TPU:0 now
where the time goes in v3:
time: 20.4 us; the launch traced here: 20.1 us
  Pallas kernels  17.7 us (87%)
  local copies, waits for them, and re-layouts  1.83 us (9%)
  between operations  0.65 us (3%)
    pallas_call x1, Pallas kernels, per_device(): pl.pallas_call(functools.partial(messages_kernel, tiles, groups, cols, D)...  12.8 us
    pallas_call x1, Pallas kernels, per_device(): pl.pallas_call(functools.partial(gates_kernel, cols, D), out_shape=(jax.S...  4.83 us
    unnamed x4, local copies, waits for them, and re-layouts  1.83 us

profile of v3, /device:TPU:0, one launch (start us, length us, event | category | flops | bytes accessed | tf_op | source)
XLA Modules:
  0.0 20.1 jit_solution(18372510365633125723)
XLA Ops:
  0.6 0.0 copy-start
  0.6 1.1 %copy-done = bf16[1,3,2,65536]{3,2,1,0:T(2,128)(2,1)S(1)} copy-done((bf16[1,3,2,65536]{3,2,1,0:T(2,128)(2,1)S(1)}, bf16[1,3,2,65536]{3,2,1,0:T(2,128)(2,1)}, u32[]{:S(2)}) %copy-start) | copy-done | bytes 786456
  1.8 0.0 copy-start.1
  1.8 0.7 %copy-done.1 = f32[1,3,4,256]{3,2,1,0:T(4,128)S(1)} copy-done((f32[1,3,4,256]{3,2,1,0:T(4,128)S(1)}, f32[1,3,4,256]{3,2,1,0:T(4,128)}, u32[]{:S(2)}) %copy-start.1) | copy-done | bytes 12312
  2.5 12.8 %shard_map.41 = (bf16[3,2,256,256]{3,2,1,0:T(8,128)(2,1)S(1)}, f32[3,16,192]{2,1,0:T(8,128)S(1)}, f32[192,16]{1,0:T(8,128)S(1)}) custom-call(bf16[3,1024,128]{2,1,0:T(8,128)(2,1)S(1)} %bitcast.12, f32[3,4,256]{2,1,0:T(4,128)S(1)} %bitcast.13), custom_call_target="tpu_custom_call" | custom-call | tf_op jit(solution)/shard_map/pallas_call | solution.py:506
  15.3 4.8 %shard_map.42 = (bf16[3,1024,128]{2,1,0:T(8,128)(2,1)}, f32[3,4,256]{2,1,0:T(4,128)}) custom-call(bf16[3,2,256,256]{3,2,1,0:T(8,128)(2,1)S(1)} %get-tuple-element.7.ax_ref, f32[3,16,192]{2,1,0:T(8,128)S(1)} %get-tuple-element.8.env_ref, f32[192,16]{1,0:T(8,128)S(1)} %get-tuple-element.9.in_ref), custom_call_target="tpu_custom_call" | custom-call | tf_op jit(solution)/shard_map/pallas_call | solution.py:530
Async XLA Ops:
  0.6 1.1 %copy-start = (bf16[1,3,2,65536]{3,2,1,0:T(2,128)(2,1)S(1)}, bf16[1,3,2,65536]{3,2,1,0:T(2,128)(2,1)}, u32[]{:S(2)}) copy-start(bf16[1,3,2,65536]{3,2,1,0:T(2,128)(2,1)} %param.2) | copy-start | bytes 2359300
  1.8 0.7 %copy-start.1 = (f32[1,3,4,256]{3,2,1,0:T(4,128)S(1)}, f32[1,3,4,256]{3,2,1,0:T(4,128)}, u32[]{:S(2)}) copy-start(f32[1,3,4,256]{3,2,1,0:T(4,128)} %param.3) | copy-start | bytes 36868
